TPU v7x, 128 devices: a whole 4x4x4 slice. The times are simulated.
128 devices in a mesh: rep: 8 (over y, z_lo), tp: 16 (over x, z_hi, core).
Axes of the slice: x: 4, y: 4, z: 4 (z_hi: 2, z_lo: 2; z = z_hi * 2 + z_lo), core: 2. Of those that a mesh axis runs over, the one named last changes fastest.
Arguments:
- embeds: bfloat16 [6272, 5120], P('rep', 'tp'), parts along dimension 0, may hold values from -6 to 6
- remask: int32 [6272], P('rep'), parts along dimension 0, may hold values 0 or 1
- lengths: int32 [32], P('rep'), parts along dimension 0, may hold values from 49 to 196, as said below
- mask_vec: bfloat16 [5120], P('tp'), may hold values from -6 to 6
- attn_gain: bfloat16 [5120], replicated, may hold values from 0.25 to 1.75
- w_query: bfloat16 [5120, 4096], P(None, 'tp'), may hold values from -0.078125 to 0.078125
- q_bias: bfloat16 [4096], P('tp'), may hold values from -200 to 200
- w_key: bfloat16 [5120, 1024], P(None, 'tp'), may hold values from -0.078125 to 0.078125
- w_value: bfloat16 [5120, 1024], P(None, 'tp'), may hold values from -0.078125 to 0.078125
- v_bias: bfloat16 [1024], P('tp'), may hold values from -3 to 3
- w_out: bfloat16 [4096, 5120], P('tp'), may hold values from -0.125 to 0.125
- head_gain: bfloat16 [5120], replicated, may hold values from 0.25 to 1.75
- w_head: bfloat16 [5120, 512], P(None, 'tp'), may hold values from -20 to 20
Outputs:
- hidden: bfloat16 [6272, 5120], P('rep', 'tp'), parts along dimension 0
- logprob: float32 [6272, 512], P('rep', 'tp'), parts along dimension 0
There are 8 independent parts, one for each index of `rep`. A program takes and returns all parts, laid end to end along the dimension named above; an argument that names none is the same for every part. Nothing has to cross between parts.
Inputs may be any that keep to these rules, and one draw needn't show every extreme that they name: `lengths`: every request has at least 49 tokens, and one request of each part has exactly 196.
All inputs are finite; a program needn't handle non-finite values.
Results may differ from a plain program's by a relative error of at most 0.018.
The roundings to bfloat16 on the way count: a program that leaves them out, or rounds other values in their place, can miss the bound.
Values may be sent and summed in bfloat16 or wider, within the bound.
A program may use at most 128 MiB of HBM per device.

v0:
```python
import jax
import jax.numpy as jnp
from jax import lax
from jax.sharding import PartitionSpec as P

HS = 128
L = 196
EPS = 1e-06


def swapped(value, axis, apart):
    mask = 2**apart
    pairs = [(source, source ^ mask) for source in range(lax.axis_size(axis))]
    return lax.ppermute(value, axis, pairs)


def combined_all(x, axis, combine):
    everything = jax.tree.map(lambda part: lax.all_gather(part, axis), x)
    initial = jax.tree.map(lambda part: part[0], everything)

    def lap(k, so_far):
        return combine(so_far, jax.tree.map(lambda part: part[k], everything))

    return lax.fori_loop(1, lax.axis_size(axis), lap, initial)


def rms_norm(matrix, gain):
    wide = matrix.astype(jnp.float32)
    inverse = lax.rsqrt(jnp.mean(wide * wide, axis=-1, keepdims=True) + EPS)
    return (wide * inverse * gain.astype(jnp.float32)).astype(jnp.bfloat16)


def combine_pair(first_pair, second_pair):
    top = jnp.maximum(first_pair[0], second_pair[0])
    total = first_pair[1] * jnp.exp(first_pair[0] - top) + second_pair[1] * jnp.exp(
        second_pair[0] - top
    )
    return (top, total)


def on_device(
    embeds,
    remask,
    lengths,
    mask_vec,
    attn_gain,
    w_query,
    q_bias,
    w_key,
    w_value,
    v_bias,
    w_out,
    head_gain,
    w_head,
):
    requests = lengths.shape[0]
    tokens_all = embeds.shape[0]
    masked_local = jnp.where(remask[:, None] == 1, mask_vec[None, :], embeds)
    gathered = lax.all_gather(masked_local, "tp", axis=1, tiled=True)
    normed = rms_norm(gathered, attn_gain)
    queries = (
        jnp.dot(normed, w_query, preferred_element_type=jnp.float32) + q_bias.astype(jnp.float32)
    ).astype(jnp.bfloat16)
    key_rows = jnp.dot(normed, w_key, preferred_element_type=jnp.float32).astype(jnp.bfloat16)
    value_rows = (
        jnp.dot(normed, w_value, preferred_element_type=jnp.float32) + v_bias.astype(jnp.float32)
    ).astype(jnp.bfloat16)
    my_index = lax.axis_index("tp")
    other_key, other_value = swapped((key_rows, value_rows), "tp", 0)
    lower = jnp.bitwise_and(jnp.right_shift(my_index, 0), 1) == 0
    key_rows = jnp.where(
        lower,
        jnp.concatenate([key_rows, other_key], axis=1),
        jnp.concatenate([other_key, key_rows], axis=1),
    )
    value_rows = jnp.where(
        lower,
        jnp.concatenate([value_rows, other_value], axis=1),
        jnp.concatenate([other_value, value_rows], axis=1),
    )
    heads_dev = queries.shape[1] // HS
    kv_count = key_rows.shape[1] // HS
    repeats = heads_dev // kv_count
    k_four = jnp.repeat(key_rows.reshape(requests, L, kv_count, HS), repeats, axis=2)
    v_four = jnp.repeat(value_rows.reshape(requests, L, kv_count, HS), repeats, axis=2)
    q_four = queries.reshape(requests, L, heads_dev, HS)
    scores = jnp.einsum(
        "rqhd,rkhd->rhqk", q_four, k_four, preferred_element_type=jnp.float32
    ) * HS ** (-0.5)
    valid = jnp.arange(L, dtype=jnp.int32)[None, :] < lengths[:, None]
    scores = jnp.where(valid[:, None, None, :], scores, jnp.float32(-1e30))
    peak = jnp.max(scores, axis=-1, keepdims=True)
    expo = jnp.exp(scores - peak)
    attn_prob = (expo / jnp.sum(expo, axis=-1, keepdims=True)).astype(jnp.bfloat16)
    context = jnp.einsum(
        "rhqk,rkhd->rqhd", attn_prob, v_four, preferred_element_type=jnp.float32
    ).astype(jnp.bfloat16)
    context = context.reshape(tokens_all, heads_dev * HS)
    portion = lax.psum_scatter(
        lax.dot_general(
            w_out, context, (((0,), (1,)), ((), ())), preferred_element_type=jnp.float32
        ).astype(jnp.bfloat16),
        "tp",
        scatter_dimension=0,
        tiled=True,
    ).astype(jnp.float32)
    hidden_local = (masked_local.astype(jnp.float32) + portion.T).astype(jnp.bfloat16)
    hidden_full = lax.all_gather(hidden_local, "tp", axis=1, tiled=True)
    normed_head = rms_norm(hidden_full, head_gain)
    logits = jnp.dot(normed_head, w_head, preferred_element_type=jnp.float32)
    local_top = jnp.max(logits, axis=-1)
    local_total = jnp.sum(jnp.exp(logits - local_top[:, None]), axis=-1)
    row_top, row_total = combined_all((local_top, local_total), "tp", combine_pair)
    log_total = row_top + jnp.log(row_total)
    return (hidden_local, logits - log_total[:, None])


def solution(mesh):
    placed = (
        P("rep", "tp"),
        P("rep"),
        P("rep"),
        P("tp"),
        P(),
        P(None, "tp"),
        P("tp"),
        P(None, "tp"),
        P(None, "tp"),
        P("tp"),
        P("tp", None),
        P(),
        P(None, "tp"),
    )
    return jax.shard_map(
        on_device,
        mesh=mesh,
        in_specs=placed,
        out_specs=(P("rep", "tp"), P("rep", "tp")),
        check_vma=False,
    )
```

profile of v0, /device:TPU:0, one launch (start us, length us, event | category | flops | bytes accessed | tf_op | source)
XLA Modules:
  0.0 478.5 jit_solution(16068774313407309099)
XLA Ops:
  7.2 0.8 broadcast_compare_fusion
  8.1 2.0 broadcast_select_fusion
  10.1 0.7 convert_element_type.57
  10.9 0.7 convert_element_type.59
  11.5 0.7 convert_element_type.61
  12.2 0.7 iota_compare_fusion
  12.9 76.6 %all-gather.5.cloned.1.call-done = bf16[784,5120]{0,1:T(8,128)(2,1)} async-done(((bf16[784,320]{0,1:T(8,128)(2,1)}), bf16[784,5120]{0,1:T(8,128)(2,1)}) %all-gather.5.cloned.1.call-update) | async-done | bytes 8028176 | tf_op jit(solution)/shard_map/all_gather | solution.py:59
  89.5 5.5 %fusion.1 = f32[784]{0:T(1024)S(1)} fusion(bf16[784,5120]{0,1:T(8,128)(2,1)} %all-gather.5.cloned.1.call-done), kind=kLoop, calls=%fused_computation.8 | loop fusion | flops 12041456 | bytes 8031296 | tf_op jit(solution)/shard_map/reduce_sum | solution.py:29
  95.1 9.4 %fusion.3 = bf16[784,5120]{0,1:T(8,128)(2,1)} fusion(bf16[784,5120]{0,1:T(8,128)(2,1)} %all-gather.5.cloned.1.call-done, f32[5120]{0:T(1024)S(1)} %convert_element_type.57, f32[784]{0:T(1024)S(1)} %add_rsqrt_fusion.1), kind=kLoop, calls=%fused_computation.10 | loop fusion | flops 16056320 | bytes 16079936 | tf_op jit(solution)/shard_map/convert_element_type | solution.py:30
  104.4 5.3 %fusion.15 = bf16[784,64]{0,1:T(8,128)(2,1)S(1)} fusion(bf16[5120,64]{0,1:T(8,128)(2,1)S(1)} %copy-done.5, bf16[784,5120]{0,1:T(8,128)(2,1)} %fusion.3, f32[64]{0:T(128)S(1)} %convert_element_type.59), kind=kOutput, calls=%fused_computation.28 | convolution fusion | flops 513902592 | bytes 8784128 | tf_op jit(solution)/shard_map/dot_general | solution.py:66
  109.7 0.3 collective-permute-start
  110.1 0.6 copy-done.1
  110.7 0.1 copy-done.6
  110.7 1.5 convolution_convert_fusion.2
  112.3 0.5 collective-permute-start.1
  112.8 2.6 fusion.13
  115.4 0.1 concatenate.28
  115.6 0.1 concatenate.32
  115.7 0.8 reshape.89
  116.6 1.0 concatenate.29
  117.6 1.7 concatenate.33
  119.3 1.6 maximum_select_fusion
  121.0 0.2 copy.29
  121.2 0.2 copy.28
  121.4 2.9 exponential_reduce_fusion
  124.3 1.9 fusion.14
  126.2 0.3 copy.32
  126.6 5.4 %fusion.11 = bf16[5120,784]{0,1:T(8,128)(2,1)} fusion(bf16[256,5120]{1,0:T(8,128)(2,1)S(1)} %copy-done, bf16[98,8,2,128]{3,2,1,0:T(2,128)(2,1)S(1)} %bitcast.31), kind=kOutput, calls=%fused_computation.18 | convolution fusion | flops 2059223040 | bytes 11051008 | tf_op jit(solution)/shard_map/dot_general | solution.py:100
  132.0 12.6 %copy.35 = bf16[5120,784]{1,0:T(8,128)(2,1)} copy(bf16[5120,784]{0,1:T(8,128)(2,1)} %fusion.11) | data formatting | bytes 16056320
  144.6 103.8 %reduce-scatter.4.cloned.1.call-done = bf16[320,784]{1,0:T(8,128)(2,1)} async-done(((bf16[5120,784]{1,0:T(8,128)(2,1)}), bf16[320,784]{1,0:T(8,128)(2,1)}) %reduce-scatter.4.cloned.1.call-update) | async-done | bytes 501776 | tf_op jit(solution)/shard_map/reduce_scatter | solution.py:99
  248.4 2.1 fusion.16
  250.6 0.3 all-reduce.5.cloned.1.call-start
  250.9 0.6 dynamic-slice
  252.1 74.0 %all-gather.7.cloned.1.call-done = bf16[784,5120]{0,1:T(8,128)(2,1)} async-done(((bf16[784,320]{0,1:T(8,128)(2,1)}), bf16[784,5120]{0,1:T(8,128)(2,1)}) %all-gather.7.cloned.1.call-update) | async-done | bytes 8028176 | tf_op jit(solution)/shard_map/all_gather | solution.py:108
  326.1 5.7 %fusion.4 = f32[784]{0:T(1024)S(1)} fusion(bf16[784,5120]{0,1:T(8,128)(2,1)} %all-gather.7.cloned.1.call-done), kind=kLoop, calls=%fused_computation.11 | loop fusion | flops 12041456 | bytes 8031296 | tf_op jit(solution)/shard_map/reduce_sum | solution.py:29
  331.8 0.5 copy-done.2
  332.3 2.7 fusion.37
  335.1 0.3 dynamic-update-slice
  335.4 0.3 dynamic-update-slice.1
  335.7 0.3 copy-done.8
  336.0 0.3 copy-done.7
  336.3 130.7 %all-reduce.5.cloned.1.call-done = (f32[12544]{0:T(1024)}, f32[12544]{0:T(1024)}) async-done(((f32[12544]{0:T(1024)}, f32[12544]{0:T(1024)}), (f32[12544]{0:T(1024)}, f32[12544]{0:T(1024)})) %all-reduce.5.cloned.1.call-update) | async-done | bytes 100368
  467.0 0.9 reshape.92
  467.9 0.7 slice.10
  468.6 0.9 reshape.93
  469.5 0.7 slice.11
  470.2 1.1 while.17
  471.3 0.7 broadcast_subtract_fusion
  (67 shorter events, 1.0 us)
Async XLA Ops:
  7.2 119.4 %copy-start = (bf16[256,5120]{1,0:T(8,128)(2,1)S(1)}, bf16[256,5120]{1,0:T(8,128)(2,1)}, u32[]{:S(2)}) copy-start(bf16[256,5120]{1,0:T(8,128)(2,1)} %param.25) | copy-start | bytes 7864324
  7.2 82.3 %all-gather.5.cloned.1.call-start = ((), (), s32[]{:S(2)}) async-start(), calls=%async_computation.1 | async-start | bytes 9748480 | tf_op jit(solution)/shard_map/all_gather | solution.py:59
  10.1 238.3 %reduce-scatter.4.cloned.1.call-start = ((), (), s32[]{:S(2)}) async-start(), calls=%async_computation.3 | async-start | bytes 9748480 | tf_op jit(solution)/shard_map/reduce_scatter | solution.py:99
  95.1 9.4 %copy-start.5 = (bf16[5120,64]{0,1:T(8,128)(2,1)S(1)}, bf16[5120,64]{0,1:T(8,128)(2,1)}, u32[]{:S(2)}) copy-start(bf16[5120,64]{0,1:T(8,128)(2,1)} %param.23) | copy-start | bytes 1966084
  104.4 6.2 %copy-start.1 = (bf16[784,5120]{0,1:T(8,128)(2,1)S(1)}, bf16[784,5120]{0,1:T(8,128)(2,1)}, u32[]{:S(2)}) copy-start(bf16[784,5120]{0,1:T(8,128)(2,1)} %fusion.3) | copy-start | bytes 24084484
  104.4 6.3 %copy-start.6 = (bf16[5120,64]{0,1:T(8,128)(2,1)S(1)}, bf16[5120,64]{0,1:T(8,128)(2,1)}, u32[]{:S(2)}) copy-start(bf16[5120,64]{0,1:T(8,128)(2,1)} %param.22) | copy-start | bytes 1966084
  109.7 3.1 copy-start.3
  109.7 6.8 %collective-permute-start = (bf16[784,64]{0,1:T(8,128)(2,1)S(1)}, bf16[784,64]{0,1:T(8,128)(2,1)}, u32[]{:S(2)}, u32[]{:S(2)}) collective-permute-start(bf16[784,64]{0,1:T(8,128)(2,1)S(1)} %fusion.15), channel_id=1, source_target_pairs={{0,1},{1,0},{2,3},{3,2},{4,5},{5,4},{6,7},{7,6},{8,9},{9,8},{10,11... | collective-permute-start | bytes 301064 | tf_op jit(solution)/shard_map/ppermute | solution.py:14
  112.3 5.3 %collective-permute-start.1 = (bf16[784,64]{0,1:T(8,128)(2,1)S(1)}, bf16[784,64]{0,1:T(8,128)(2,1)}, u32[]{:S(2)}, u32[]{:S(2)}) collective-permute-start(bf16[784,64]{0,1:T(8,128)(2,1)S(1)} %convolution_convert_fusion.2), channel_id=1, source_target_pairs={{0,1},{1,0},{2,3},{3,2},{4,5},{5,4},{6,7},{7,6},{8,9},{9,8},{10,11... | collective-permute-start | bytes 301064 | tf_op jit(solution)/shard_map/ppermute | solution.py:14
  131.9 116.5 %copy-start.4 = (bf16[784,320]{0,1:T(8,128)(2,1)S(1)}, bf16[784,320]{0,1:T(8,128)(2,1)}, u32[]{:S(2)}) copy-start(bf16[784,320]{0,1:T(8,128)(2,1)} %param.15) | copy-start | bytes 1505284
  131.9 116.5 %copy-start.10 = (bf16[320]{0:T(512)(128)(2,1)S(1)}, bf16[320]{0:T(512)(128)(2,1)}, u32[]{:S(2)}) copy-start(bf16[320]{0:T(512)(128)(2,1)} %param.18) | copy-start | bytes 1924
  144.5 106.3 %copy-start.9 = (bf16[5120]{0:T(1024)(128)(2,1)S(1)}, bf16[5120]{0:T(1024)(128)(2,1)}, u32[]{:S(2)}) copy-start(bf16[5120]{0:T(1024)(128)(2,1)} %param.26) | copy-start | bytes 30724
  144.5 106.3 %copy-start.12 = (u32[128]{0:T(128)S(1)}, u32[128]{0:T(128)}, u32[]{:S(2)}) copy-start(u32[128]{0:T(128)} %constant.61) | copy-start | bytes 1540
  144.5 187.3 %copy-start.11 = (bf16[5120,32]{0,1:T(8,128)(2,1)S(1)}, bf16[5120,32]{0,1:T(8,128)(2,1)}, u32[]{:S(2)}) copy-start(bf16[5120,32]{0,1:T(8,128)(2,1)} %param.27) | copy-start | bytes 983044
  144.6 181.5 %all-gather.7.cloned.1.call-start = ((), (), s32[]{:S(2)}) async-start(), calls=%async_computation.2 | async-start | bytes 9748480 | tf_op jit(solution)/shard_map/all_gather | solution.py:108
  250.6 216.4 %all-reduce.5.cloned.1.call-start = ((), (), s32[]{:S(2)}) async-start(), calls=%async_computation.4 | async-start | bytes 212992
  326.1 6.2 %copy-start.2 = (bf16[784,5120]{0,1:T(8,128)(2,1)S(1)}, bf16[784,5120]{0,1:T(8,128)(2,1)}, u32[]{:S(2)}) copy-start(bf16[784,5120]{0,1:T(8,128)(2,1)} %all-gather.7.cloned.1.call-done) | copy-start | bytes 24084484
  335.4 0.6 copy-start.8
  335.7 0.6 copy-start.7
Sparse Core Ops, SparseCore 0:
  11.0 78.4 all-gather.4
  144.7 103.6 reduce-scatter.3
  251.4 74.6 all-gather.6
  336.5 130.4 all-reduce.4
where the time goes:
time: 479 us; the launch traced here: 478 us
  waiting for transfers between devices  385 us (80%)
  other arithmetic  30.8 us (6%)
  local copies, waits for them, and re-layouts  23.9 us (5%)
  matrix products  22.3 us (5%)
  between operations  14.6 us (3%)
    unnamed x5, waiting for transfers between devices  131 us
    reduce_scatter x1, waiting for transfers between devices, on_device(): lax.psum_scatter(lax.dot_general(w_out, context, (((0,), (1,)), ((), ()))...  104 us
    all_gather x1, waiting for transfers between devices, on_device(): gathered = lax.all_gather(masked_local, 'tp', axis=1, tiled=True)  76.6 us
    all_gather x1, waiting for transfers between devices, on_device(): hidden_full = lax.all_gather(hidden_local, 'tp', axis=1, tiled=True)  74 us
    unnamed x32, local copies, waits for them, and re-layouts  15.6 us
    reduce_sum x2, other arithmetic, rms_norm(): inverse = lax.rsqrt(jnp.mean(wide * wide, axis=-1, keepdims=True) + EPS)  11.2 us
    convert_element_type x3, other arithmetic, rms_norm(): return (wide * inverse * gain.astype(jnp.float32)).astype(jnp.bfloat16)  10.1 us
  transfers between devices with their start and end apart: 6, of which 4 were waited for; matrix products, arithmetic and copies ran while one was open for 2% of the time, Pallas kernels for 0%

commit v1 on v0

--- a/solution.py
+++ b/solution.py
@@ -56,7 +56,9 @@
     requests = lengths.shape[0]
     tokens_all = embeds.shape[0]
     masked_local = jnp.where(remask[:, None] == 1, mask_vec[None, :], embeds)
-    gathered = lax.all_gather(masked_local, "tp", axis=1, tiled=True)
+    gathered = jnp.concatenate(
+        lax.all_to_all(jnp.stack([masked_local] * lax.axis_size("tp")), "tp", 0, 0), axis=1
+    )
     normed = rms_norm(gathered, attn_gain)
     queries = (
         jnp.dot(normed, w_query, preferred_element_type=jnp.float32) + q_bias.astype(jnp.float32)

time: 479 us -> 604 us (1.26)
  waiting for transfers between devices: 385 us -> 458 us
  local copies, waits for them, and re-layouts: 23.9 us -> 60.9 us
  starting transfers between devices: 1.22 us -> 9.17 us
  other arithmetic: 30.8 us -> 38.1 us
    all_to_all x0 -> x1, waiting for transfers between devices: none -> 145 us  [on_device(): lax.all_to_all(jnp.stack([masked_local] * lax.axis_size('tp')), 'tp', 0, 0)]
    unnamed x5, waiting for transfers between devices: 131 us -> 239 us
    reduce_scatter x1 -> x0, waiting for transfers between devices: 104 us -> none  [on_device(): lax.psum_scatter(lax.dot_general(w_out, context, (((0,), (1,)), ((), ()))...]
    all_gather x1 -> x0, waiting for transfers between devices: 76.6 us -> none  [on_device(): gathered = lax.all_gather(masked_local, 'tp', axis=1, tiled=True)]
    convert_element_type x0 -> x1, local copies, waits for them, and re-layouts: none -> 18.8 us  [rms_norm(): wide = matrix.astype(jnp.float32)]
    convert_element_type x0 -> x1, other arithmetic: none -> 11.8 us  [rms_norm(): wide = matrix.astype(jnp.float32)]
    all_to_all x0 -> x1, starting transfers between devices: none -> 7.99 us  [on_device(): lax.all_to_all(jnp.stack([masked_local] * lax.axis_size('tp')), 'tp', 0, 0)]
    unnamed x32 -> x39, local copies, waits for them, and re-layouts: 15.6 us -> 20.6 us
where the time goes in v1:
time: 604 us; the launch traced here: 603 us
  waiting for transfers between devices  458 us (76%)
  local copies, waits for them, and re-layouts  60.9 us (10%)
  other arithmetic  38.1 us (6%)
  matrix products  21.4 us (4%)
  between operations  14.7 us (2%)
  starting transfers between devices  9.17 us (2%)
    unnamed x5, waiting for transfers between devices  239 us
    all_to_all x1, waiting for transfers between devices, on_device(): lax.all_to_all(jnp.stack([masked_local] * lax.axis_size('tp')), 'tp', 0, 0)  145 us
    all_gather x1, waiting for transfers between devices, on_device(): hidden_full = lax.all_gather(hidden_local, 'tp', axis=1, tiled=True)  73.2 us
    unnamed x39, local copies, waits for them, and re-layouts  20.6 us
    convert_element_type x1, local copies, waits for them, and re-layouts, rms_norm(): wide = matrix.astype(jnp.float32)  18.8 us
  transfers between devices with their start and end apart: 6, of which 4 were waited for; matrix products, arithmetic and copies ran while one was open for 2% of the time, Pallas kernels for 0%

profile of v1, /device:TPU:0, one launch (start us, length us, event | category | flops | bytes accessed | tf_op | source)
XLA Modules:
  0.0 602.8 jit_solution(16702483539432785706)
XLA Ops:
  7.2 0.8 broadcast_compare_fusion
  8.0 1.4 copy.28
  9.4 1.7 broadcast_select_fusion
  11.1 2.1 copy.29
  13.2 5.9 stack.2
  19.1 8.0 %all-to-all-start = ((bf16[16,784,320]{1,2,0:T(8,128)(2,1)}), bf16[16,784,320]{1,2,0:T(8,128)(2,1)}, u32[]{:S(2)}, u32[]{:S(2)}) async-start(bf16[16,784,320]{1,2,0:T(8,128)(2,1)} %stack.2), calls=%async_computation | async-start | bytes 18350080 | tf_op jit(solution)/shard_map/all_to_all | solution.py:60
  27.3 145.4 %all-to-all-done = bf16[16,784,320]{1,2,0:T(8,128)(2,1)} async-done(((bf16[16,784,320]{1,2,0:T(8,128)(2,1)}), bf16[16,784,320]{1,2,0:T(8,128)(2,1)}, u32[]{:S(2)}, u32[]{:S(2)}) %all-to-all-start) | async-done | bytes 8028192 | tf_op jit(solution)/shard_map/all_to_all | solution.py:60
  172.7 5.5 multiply_reduce_fusion
  178.3 11.8 %convert_element_type.87 = f32[16,784,320]{1,2,0:T(8,128)} convert(bf16[16,784,320]{1,2,0:T(8,128)(2,1)} %all-to-all-done) | non-fusion elementwise | flops 4014080 | bytes 24084480 | tf_op jit(solution)/shard_map/convert_element_type | solution.py:28
  190.1 18.8 %copy.39 = f32[784,5120]{1,0:T(8,128)} copy(f32[784,5120]{0,1:T(8,128)} %bitcast.34) | data formatting | bytes 32112640 | tf_op jit(solution)/shard_map/convert_element_type | solution.py:28
  208.9 6.8 %multiply_convert_fusion = bf16[784,5120]{1,0:T(8,128)(2,1)S(1)} fusion(f32[784,5120]{1,0:T(8,128)} %copy.39, f32[5120]{0:T(1024)S(1)} %convert_element_type.70, f32[784]{0:T(1024)S(1)} %add_rsqrt_fusion.1), kind=kLoop, calls=%fused_computation.10 | loop fusion | flops 12042240 | bytes 24108096 | tf_op jit(solution)/shard_map/convert_element_type | solution.py:30
  215.7 2.7 convolution_convert_fusion.2
  218.5 2.7 fusion.13
  221.2 0.7 collective-permute-start
  221.9 3.0 fusion.10
  224.9 0.8 concatenate.32
  225.7 0.8 concatenate.28
  226.5 1.8 reshape.95
  228.4 1.7 concatenate.33
  230.1 1.7 concatenate.29
  231.8 2.6 maximum_select_fusion
  234.4 1.8 copy.31
  236.2 0.9 copy.32
  237.1 2.9 exponential_reduce_fusion
  240.0 2.0 fusion.11
  242.1 0.3 copy.35
  242.4 5.4 fusion.8
  247.8 12.5 %copy.40 = bf16[5120,784]{1,0:T(8,128)(2,1)} copy(bf16[5120,784]{0,1:T(8,128)(2,1)} %fusion.8) | data formatting | bytes 16056320
  260.4 108.6 %reduce-scatter.4.cloned.1.call-done = bf16[320,784]{1,0:T(8,128)(2,1)} async-done(((bf16[5120,784]{1,0:T(8,128)(2,1)}), bf16[320,784]{1,0:T(8,128)(2,1)}) %reduce-scatter.4.cloned.1.call-update) | async-done | bytes 501776
  369.0 2.1 copy.41
  371.2 2.2 fusion.12
  373.3 2.2 copy.37
  375.8 0.6 dynamic-slice
  377.1 73.2 %all-gather.4.cloned.1.call-done = bf16[784,5120]{0,1:T(8,128)(2,1)} async-done(((bf16[784,320]{0,1:T(8,128)(2,1)}), bf16[784,5120]{0,1:T(8,128)(2,1)}) %all-gather.4.cloned.1.call-update) | async-done | bytes 8028176 | tf_op jit(solution)/shard_map/all_gather | solution.py:110
  450.3 5.7 fusion.1
  456.0 0.5 copy-done.1
  456.5 2.7 fusion.34
  459.3 0.3 dynamic-update-slice
  459.6 0.3 dynamic-update-slice.1
  459.9 0.3 copy-done.5
  460.2 0.3 copy-done.4
  460.5 130.8 %all-reduce.5.cloned.1.call-done = (f32[12544]{0:T(1024)}, f32[12544]{0:T(1024)}) async-done(((f32[12544]{0:T(1024)}, f32[12544]{0:T(1024)}), (f32[12544]{0:T(1024)}, f32[12544]{0:T(1024)})) %all-reduce.5.cloned.1.call-update) | async-done | bytes 100368
  591.3 0.7 slice.10
  592.0 0.9 reshape.99
  592.9 0.7 slice.11
  593.6 0.9 reshape.100
  594.5 1.1 while.17
  595.6 0.7 broadcast_subtract_fusion
  (77 shorter events, 1.4 us)
Async XLA Ops:
  7.2 235.3 %copy-start = (bf16[256,5120]{1,0:T(8,128)(2,1)S(1)}, bf16[256,5120]{1,0:T(8,128)(2,1)}, u32[]{:S(2)}) copy-start(bf16[256,5120]{1,0:T(8,128)(2,1)} %param.25) | copy-start | bytes 7864324
  19.1 8.1 %copy-start.11 = (bf16[64]{0:T(256)(128)(2,1)S(1)}, bf16[64]{0:T(256)(128)(2,1)}, u32[]{:S(2)}) copy-start(bf16[64]{0:T(256)(128)(2,1)} %param.24) | copy-start | bytes 388
  19.1 8.1 %copy-start.12 = (bf16[256]{0:T(256)(128)(2,1)S(1)}, bf16[256]{0:T(256)(128)(2,1)}, u32[]{:S(2)}) copy-start(bf16[256]{0:T(256)(128)(2,1)} %param.21) | copy-start | bytes 1540
  19.1 8.1 %copy-start.6 = (bf16[5120]{0:T(1024)(128)(2,1)S(1)}, bf16[5120]{0:T(1024)(128)(2,1)}, u32[]{:S(2)}) copy-start(bf16[5120]{0:T(1024)(128)(2,1)} %param.19) | copy-start | bytes 30724
  19.1 8.1 %copy-start.13 = (s32[4]{0:T(128)S(1)}, s32[4]{0:T(128)}, u32[]{:S(2)}) copy-start(s32[4]{0:T(128)} %param.17) | copy-start | bytes 52
  19.1 153.6 %all-to-all-start = ((bf16[16,784,320]{1,2,0:T(8,128)(2,1)}), bf16[16,784,320]{1,2,0:T(8,128)(2,1)}, u32[]{:S(2)}, u32[]{:S(2)}) async-start(bf16[16,784,320]{1,2,0:T(8,128)(2,1)} %stack.2), calls=%async_computation | async-start | bytes 18350080 | tf_op jit(solution)/shard_map/all_to_all | solution.py:60
  27.1 342.0 %reduce-scatter.4.cloned.1.call-start = ((), (), s32[]{:S(2)}) async-start(), calls=%async_computation.3 | async-start | bytes 9748480
  208.9 6.8 %copy-start.2 = (bf16[5120,64]{0,1:T(8,128)(2,1)S(1)}, bf16[5120,64]{0,1:T(8,128)(2,1)}, u32[]{:S(2)}) copy-start(bf16[5120,64]{0,1:T(8,128)(2,1)} %param.22) | copy-start | bytes 1966084
  215.7 2.8 copy-start.3
  218.4 3.5 copy-start.9
  218.4 10.0 %collective-permute-start.1 = (bf16[784,64]{0,1:T(8,128)(2,1)S(1)}, bf16[784,64]{0,1:T(8,128)(2,1)}, u32[]{:S(2)}, u32[]{:S(2)}) collective-permute-start(bf16[784,64]{0,1:T(8,128)(2,1)S(1)} %convolution_convert_fusion.2), channel_id=1, source_target_pairs={{0,1},{1,0},{2,3},{3,2},{4,5},{5,4},{6,7},{7,6},{8,9},{9,8},{10,11... | collective-permute-start | bytes 301064 | tf_op jit(solution)/shard_map/ppermute | solution.py:14
  221.2 8.9 %collective-permute-start = (bf16[784,64]{0,1:T(8,128)(2,1)S(1)}, bf16[784,64]{0,1:T(8,128)(2,1)}, u32[]{:S(2)}, u32[]{:S(2)}) collective-permute-start(bf16[784,64]{0,1:T(8,128)(2,1)S(1)} %fusion.13), channel_id=1, source_target_pairs={{0,1},{1,0},{2,3},{3,2},{4,5},{5,4},{6,7},{7,6},{8,9},{9,8},{10,11... | collective-permute-start | bytes 301064 | tf_op jit(solution)/shard_map/ppermute | solution.py:14
  260.4 110.8 %copy-start.8 = (bf16[320]{0:T(512)(128)(2,1)S(1)}, bf16[320]{0:T(512)(128)(2,1)}, u32[]{:S(2)}) copy-start(bf16[320]{0:T(512)(128)(2,1)} %param.18) | copy-start | bytes 1924
  260.4 115.4 %copy-start.7 = (bf16[5120]{0:T(1024)(128)(2,1)S(1)}, bf16[5120]{0:T(1024)(128)(2,1)}, u32[]{:S(2)}) copy-start(bf16[5120]{0:T(1024)(128)(2,1)} %param.26) | copy-start | bytes 30724
  260.4 115.5 %copy-start.14 = (u32[128]{0:T(128)S(1)}, u32[128]{0:T(128)}, u32[]{:S(2)}) copy-start(u32[128]{0:T(128)} %constant.61) | copy-start | bytes 1540
  260.4 189.9 %all-gather.4.cloned.1.call-start = ((), (), s32[]{:S(2)}) async-start(), calls=%async_computation.2 | async-start | bytes 9748480 | tf_op jit(solution)/shard_map/all_gather | solution.py:110
  373.3 82.7 %copy-start.10 = (bf16[5120,32]{0,1:T(8,128)(2,1)S(1)}, bf16[5120,32]{0,1:T(8,128)(2,1)}, u32[]{:S(2)}) copy-start(bf16[5120,32]{0,1:T(8,128)(2,1)} %param.27) | copy-start | bytes 983044
  375.5 215.8 %all-reduce.5.cloned.1.call-start = ((), (), s32[]{:S(2)}) async-start(), calls=%async_computation.4 | async-start | bytes 212992
  450.3 6.2 %copy-start.1 = (bf16[784,5120]{0,1:T(8,128)(2,1)S(1)}, bf16[784,5120]{0,1:T(8,128)(2,1)}, u32[]{:S(2)}) copy-start(bf16[784,5120]{0,1:T(8,128)(2,1)} %all-gather.4.cloned.1.call-done) | copy-start | bytes 24084484
  459.6 0.6 copy-start.5
  459.9 0.6 copy-start.4
Sparse Core Ops, SparseCore 0:
  260.5 108.4 reduce-scatter.3
  375.6 74.5 all-gather.3
  460.6 130.6 all-reduce.4
